TPU v7x, 512 devices: a whole 4x8x8 slice. The times are simulated.
512 devices in a mesh: dp: 32 (over z, x_hi, core), fsdp: 16 (over x_lo, y).
Axes of the slice: x: 4 (x_hi: 2, x_lo: 2; x = x_hi * 2 + x_lo), y: 8, z: 8, core: 2. Of those that a mesh axis runs over, the one named last changes fastest.
Arguments:
- tokens: bfloat16 [5120, 4608], P('fsdp'), may hold values from -12 to 12
- cotangent: bfloat16 [5120, 12288], P('fsdp', 'dp'), may hold values from -0.046875 to 0.046875
- gain: float32 [4608], replicated, may hold values from 0.5 to 1.5
- master: float32 [4608, 12288], P('fsdp', 'dp'), may hold values from -0.09375 to 0.09375
- momentum: float32 [4608, 12288], P('fsdp', 'dp'), may hold values from -3 to 3
Outputs:
- new_master: float32 [4608, 12288], P('fsdp', 'dp')
- new_momentum: float32 [4608, 12288], P('fsdp', 'dp')
All inputs are finite; a program needn't handle non-finite values.
Results may differ from a plain program's by a relative error of at most 0.0024.
Values may be sent and summed in bfloat16 or wider, within the bound.
A program may use at most 64 MiB of HBM per device.

v0:
```python
import math

import jax
import jax.numpy as jnp
from jax import lax
from jax.sharding import PartitionSpec as P

FF = 12288


inv_root_two = 1.0 / math.sqrt(2.0)
inv_root_two_pi = 1.0 / math.sqrt(2.0 * math.pi)


def norm_rows(tokens, gain):
    values = tokens.astype(jnp.float32)
    meansq = jnp.mean(values * values, axis=1, keepdims=True)
    return (values * lax.rsqrt(meansq + 1e-06) * gain).astype(jnp.bfloat16)


def slope_of(pre):
    cdf = 0.5 * (1.0 + jax.scipy.special.erf(pre * inv_root_two))
    return cdf + pre * jnp.exp(-0.5 * pre * pre) * inv_root_two_pi


def local(tokens, cotangent, gain, master, momentum):
    own_rows = master.shape[0]
    own_tokens = tokens.shape[0]
    n_shard = lax.axis_size("fsdp")
    n_copy = lax.axis_size("dp")
    share = own_tokens // n_copy
    along_rows = (((0,), (0,)), ((), ()))
    along_features = (((1,), (1,)), ((), ()))
    cot = cotangent.astype(jnp.float32)

    normed = norm_rows(tokens, gain)
    weights = lax.all_gather(master.astype(jnp.bfloat16), "fsdp", axis=0, tiled=True)
    mine = lax.dynamic_slice_in_dim(normed, lax.axis_index("dp") * share, share, 0)
    some = lax.all_gather(mine, "fsdp", axis=0, tiled=True)
    gram = lax.dot_general(
        some, normed, along_features, preferred_element_type=jnp.float32
    ).astype(jnp.bfloat16)
    columns = lax.dynamic_slice_in_dim(some, lax.axis_index("fsdp") * own_rows, own_rows, 1)
    both = lax.all_gather(jnp.concatenate([gram, columns], axis=1), "dp", axis=0, tiled=True)
    both = both.reshape(n_copy, n_shard, share, own_tokens + own_rows)
    both = both.transpose(1, 0, 2, 3).reshape(n_shard * own_tokens, own_tokens + own_rows)
    gram_all = both[:, :own_tokens]
    columns_all = both[:, own_tokens:]

    def gathered(pre):
        dpre = (cot * slope_of(pre)).astype(jnp.bfloat16)
        return dpre, lax.all_gather(dpre, "fsdp", axis=0, tiled=True)

    pre = jnp.dot(normed, weights, preferred_element_type=jnp.float32)
    dpre, dpre_all = gathered(pre)
    shift = lax.dot_general(gram_all, dpre_all, along_rows, preferred_element_type=jnp.float32)
    squares = lax.psum(jnp.sum(dpre.astype(jnp.float32) * shift), ("dp", "fsdp"))
    scale = math.sqrt(FF) / 4.0 / (jnp.sqrt(jnp.maximum(squares, 0.0)) + 1e-12)
    unused, dpre_two = gathered(pre + scale * shift)
    second = lax.dot_general(columns_all, dpre_two, along_rows, preferred_element_type=jnp.float32)
    new_momentum = 0.9 * momentum + second
    new_master = master - 0.002 * new_momentum
    return (new_master, new_momentum)


def solution(mesh):
    in_specs = (P("fsdp", None), P("fsdp", "dp"), P(), P("fsdp", "dp"), P("fsdp", "dp"))
    out_specs = (P("fsdp", "dp"), P("fsdp", "dp"))
    return jax.shard_map(local, mesh=mesh, in_specs=in_specs, out_specs=out_specs, check_vma=False)
```

profile of v0, /device:TPU:1, one launch (start us, length us, event | category | flops | bytes accessed | tf_op | source)
XLA Modules:
  0.0 530.9 jit_solution(4000123411859568000)
XLA Ops:
  7.2 2.6 fusion
  9.8 2.7 fusion.2
  12.5 0.7 dynamic-slice_bitcast_fusion
  13.2 0.0 all-gather.9.cloned.1.call-start
  13.3 0.7 convert_element_type.28
  14.0 0.0 all-gather.7.cloned.1.call-start
  14.1 69.3 %all-gather.15.cloned.1.call-done = bf16[16,10,4608]{2,1,0:T(8,128)(2,1)} async-done(((bf16[1,10,4608]{2,1,0:T(8,128)(2,1)}), bf16[16,10,4608]{2,1,0:T(8,128)(2,1)}) %all-gather.15.cloned.1.call-update) | async-done | bytes 1474576 | tf_op jit(solution)/shard_map/all_gather | solution.py:39
  83.4 2.8 reshape.22
  86.1 1.0 constant_dynamic-slice_fusion
  87.2 2.6 convolution_convert_fusion
  89.8 0.8 pad_maximum_fusion
  90.6 0.0 all-gather.11.cloned.1.call-start
  90.6 71.3 %all-gather.9.cloned.1.call-done = bf16[4608,384]{1,0:T(8,128)(2,1)} async-done(((bf16[288,384]{1,0:T(8,128)(2,1)}), bf16[4608,384]{1,0:T(8,128)(2,1)}) %all-gather.9.cloned.1.call-update) | async-done | bytes 3538960 | tf_op jit(solution)/shard_map/all_gather | solution.py:37
  162.0 4.5 fusion.10
  166.6 107.2 %all-gather.7.cloned.1.call-done = bf16[5120,608]{1,0:T(8,128)(2,1)} async-done(((bf16[160,608]{1,0:T(8,128)(2,1)}), bf16[5120,608]{1,0:T(8,128)(2,1)}) %all-gather.7.cloned.1.call-update) | async-done | bytes 6225936 | tf_op jit(solution)/shard_map/all_gather | solution.py:44
  273.8 12.8 %reshape.19 = bf16[32,16,10,608]{3,2,1,0:T(8,128)(2,1)} reshape(bf16[5120,608]{1,0:T(8,128)(2,1)} %all-gather.7.cloned.1.call-done) | data formatting | bytes 12451840 | tf_op jit(solution)/shard_map/reshape | solution.py:45
  286.6 9.2 %copy.8 = bf16[16,32,10,608]{3,2,1,0:T(8,128)(2,1)} copy(bf16[16,32,10,608]{3,2,0,1:T(8,128)(2,1)} %bitcast.9) | data formatting | bytes 12451840 | tf_op jit(solution)/shard_map/transpose | solution.py:46
  295.8 13.7 %reshape.20 = bf16[5120,608]{1,0:T(8,128)(2,1)} reshape(bf16[16,32,10,608]{3,2,1,0:T(8,128)(2,1)} %copy.8) | data formatting | bytes 12451840 | tf_op jit(solution)/shard_map/reshape | solution.py:46
  309.5 31.3 %all-gather.11.cloned.1.call-done = bf16[5120,384]{1,0:T(8,128)(2,1)} async-done(((bf16[320,384]{1,0:T(8,128)(2,1)}), bf16[5120,384]{1,0:T(8,128)(2,1)}) %all-gather.11.cloned.1.call-update) | async-done | bytes 3932176 | tf_op jit(solution)/shard_map/all_gather | solution.py:52
  340.8 5.8 %multiply_reduce_fusion = (f32[]{:T(128)}, f32[320,384]{1,0:T(8,128)S(1)}) fusion(bf16[320,384]{1,0:T(8,128)(2,1)S(1)} %copy-done.3, bf16[5120,384]{1,0:T(8,128)(2,1)} %all-gather.11.cloned.1.call-done, bf16[5120,608]{1,0:T(8,128)(2,1)} %reshape.20), kind=kOutput, calls=%fused_computation.25 | convolution fusion | flops 1258659840 | bytes 8601604 | tf_op jit(solution)/shard_map/dot_general | solution.py:56
  346.6 106.9 %psum.7 = f32[]{:T(128)} all-reduce(f32[]{:T(128)} %get-tuple-element.4), channel_id=1, replica_groups=mesh['dp'=32,'fsdp'=16] {'dp','fsdp'}, use_global_device_ids=true, to_apply=%region_2.0 | all-reduce | flops 1 | bytes 8 | tf_op jit(solution)/shard_map/psum | solution.py:57
  454.2 1.0 fusion.11
  455.2 62.2 %all-gather.13.cloned.1.call-done = bf16[5120,384]{1,0:T(8,128)(2,1)} async-done(((bf16[320,384]{1,0:T(8,128)(2,1)}), bf16[5120,384]{1,0:T(8,128)(2,1)}) %all-gather.13.cloned.1.call-update) | async-done | bytes 3932176 | tf_op jit(solution)/shard_map/all_gather | solution.py:52
  517.4 7.0 %multiply_subtract_fusion = (f32[288,384]{1,0:T(8,128)}, f32[288,384]{1,0:T(8,128)}) fusion(f32[288,384]{1,0:T(8,128)S(1)} %copy-done.1, bf16[5120,384]{1,0:T(8,128)(2,1)} %all-gather.13.cloned.1.call-done, bf16[5120,608]{1,0:T(8,128)(2,1)} %reshape.20, f32[288,384]{1,0:T(8,128)S(1)} %copy-done.4), kind=kOutput, calls=%fused_computation.26 | convolution fusion | flops 1132904448 | bytes 9633792 | tf_op jit(solution)/shard_map/dot_general | solution.py:60
  (18 shorter events, 0.2 us)
Async XLA Ops:
  7.2 76.2 %all-gather.15.cloned.1.call-start = ((), (), s32[]{:S(2)}) async-start(), calls=%async_computation.4 | async-start | bytes 2506752 | tf_op jit(solution)/shard_map/all_gather | solution.py:39
  7.2 6.1 %copy-start = (f32[288,384]{1,0:T(8,128)S(1)}, f32[288,384]{1,0:T(8,128)}, u32[]{:S(2)}) copy-start(f32[288,384]{1,0:T(8,128)} %param.8) | copy-start | bytes 1327108
  13.2 148.8 %all-gather.9.cloned.1.call-start = ((), (), s32[]{:S(2)}) async-start(), calls=%async_computation.1 | async-start | bytes 3760128 | tf_op jit(solution)/shard_map/all_gather | solution.py:37
  14.0 259.8 %all-gather.7.cloned.1.call-start = ((), (), s32[]{:S(2)}) async-start(), calls=%async_computation | async-start | bytes 6758400 | tf_op jit(solution)/shard_map/all_gather | solution.py:44
  90.6 250.2 %all-gather.11.cloned.1.call-start = ((), (), s32[]{:S(2)}) async-start(), calls=%async_computation.2 | async-start | bytes 4177920 | tf_op jit(solution)/shard_map/all_gather | solution.py:52
  166.5 350.9 %all-gather.13.cloned.1.call-start = ((), (), s32[]{:S(2)}) async-start(), calls=%async_computation.3 | async-start | bytes 4177920 | tf_op jit(solution)/shard_map/all_gather | solution.py:52
  295.8 45.0 %copy-start.3 = (bf16[320,384]{1,0:T(8,128)(2,1)S(1)}, bf16[320,384]{1,0:T(8,128)(2,1)}, u32[]{:S(2)}) copy-start(bf16[320,384]{1,0:T(8,128)(2,1)} %get-tuple-element.2) | copy-start | bytes 737284
  309.5 144.8 %copy-start.2 = (bf16[320,384]{1,0:T(8,128)(2,1)S(1)}, bf16[320,384]{1,0:T(8,128)(2,1)}, u32[]{:S(2)}) copy-start(bf16[320,384]{1,0:T(8,128)(2,1)} %param.6) | copy-start | bytes 737284
  309.5 207.9 %copy-start.1 = (f32[288,384]{1,0:T(8,128)S(1)}, f32[288,384]{1,0:T(8,128)}, u32[]{:S(2)}) copy-start(f32[288,384]{1,0:T(8,128)} %param.8) | copy-start | bytes 1327108
  309.5 207.9 %copy-start.4 = (f32[288,384]{1,0:T(8,128)S(1)}, f32[288,384]{1,0:T(8,128)}, u32[]{:S(2)}) copy-start(f32[288,384]{1,0:T(8,128)} %param.9) | copy-start | bytes 1327108
Sparse Core Ops, SparseCore 0:
  13.3 69.9 all-gather.14
  86.0 75.9 all-gather.8
  165.9 107.8 all-gather.6
  276.3 64.4 all-gather.10
  455.3 62.0 all-gather.12
where the time goes:
time: 541 us; the launch traced here: 531 us
  waiting for transfers between devices  341 us (63%)
  blocking collectives  107 us (20%)
  local copies, waits for them, and re-layouts  40.2 us (7%)
  matrix products  20 us (4%)
  between operations  14.6 us (3%)
  other arithmetic  7.69 us (1%)
    all_gather x1, waiting for transfers between devices, local(): lax.all_gather(jnp.concatenate([gram, columns], axis=1), 'dp', axis=0, ti...  107 us
    psum x1, blocking collectives, local(): lax.psum(jnp.sum(dpre.astype(jnp.float32) * shift), ('dp', 'fsdp'))  107 us
    all_gather x2, waiting for transfers between devices, gathered(): return (dpre, lax.all_gather(dpre, 'fsdp', axis=0, tiled=True))  93.5 us
    all_gather x1, waiting for transfers between devices, local(): lax.all_gather(master.astype(jnp.bfloat16), 'fsdp', axis=0, tiled=True)  71.3 us
    all_gather x1, waiting for transfers between devices, local(): some = lax.all_gather(mine, 'fsdp', axis=0, tiled=True)  69.3 us
    reshape x1, local copies, waits for them, and re-layouts, local(): both.transpose(1, 0, 2, 3)  13.7 us
    reshape x1, local copies, waits for them, and re-layouts, local(): both = both.reshape(n_copy, n_shard, share, own_tokens + own_rows)  12.8 us
  transfers between devices with their start and end apart: 5, of which 5 were waited for; matrix products, arithmetic and copies ran while one was open for 9% of the time, Pallas kernels for 0%

commit v1 on v0

--- a/solution.py
+++ b/solution.py
@@ -1,8 +1,11 @@
+import functools
 import math
 
 import jax
 import jax.numpy as jnp
 from jax import lax
+from jax.experimental import pallas as pl
+from jax.experimental.pallas import tpu as pltpu
 from jax.sharding import PartitionSpec as P
 
 FF = 12288
@@ -21,6 +24,165 @@
 def slope_of(pre):
     cdf = 0.5 * (1.0 + jax.scipy.special.erf(pre * inv_root_two))
     return cdf + pre * jnp.exp(-0.5 * pre * pre) * inv_root_two_pi
+
+
+RING = 8
+MESH = pl.DeviceIdType.MESH
+
+
+def gather_kernel(cut, x_ref, o_ref, side_send, side_recv, ring_send, ring_recv, local_sem):
+    me = lax.axis_index("fsdp")
+    column = lax.div(me, RING)
+    row = lax.rem(me, RING)
+    other = 1 - column
+    side = other * RING + row
+    ring = (
+        column * RING + lax.rem(row + 1, RING),
+        column * RING + lax.rem(row + RING - 1, RING),
+    )
+    total = x_ref.shape[0]
+    part = (pl.ds(0, cut), pl.ds(cut, total - cut))
+
+    barrier = pltpu.get_barrier_semaphore()
+    for peer in (side, ring[0], ring[1]):
+        pl.semaphore_signal(barrier, inc=1, device_id={"fsdp": peer}, device_id_type=MESH)
+    pl.semaphore_wait(barrier, 3)
+
+    own = pltpu.make_async_copy(x_ref, o_ref.at[me], local_sem)
+    own.start()
+
+    started = []
+
+    def move(src, dst, send, recv, peer):
+        return pltpu.make_async_remote_copy(
+            src_ref=src,
+            dst_ref=dst,
+            send_sem=send,
+            recv_sem=recv,
+            device_id={"fsdp": peer},
+            device_id_type=MESH,
+        )
+
+    def to_side(slot, origin, half, src=None):
+        place = o_ref.at[origin, part[half]]
+        copy = move(
+            place if src is None else src, place, side_send.at[slot], side_recv.at[slot], side
+        )
+        copy.start()
+        started.append(copy)
+
+    def to_ring(unit, way, hop, origin, half, src=None):
+        place = o_ref.at[origin, part[half]]
+        at = (unit * 2 + way) * 4 + hop - 1
+        copy = move(
+            place if src is None else src, place, ring_send.at[at], ring_recv.at[at], ring[way]
+        )
+        copy.start()
+        started.append(copy)
+
+    hops = ((4, 3), (3, 4), (4, 3))
+    halves = (0, 1, 1)
+    columns = (column, column, other)
+
+    first, second = x_ref.at[part[0]], x_ref.at[part[1]]
+    to_side(0, me, 1, second)
+    for way in range(2):
+        to_ring(1, way, 1, me, 1, second)
+    for way in range(2):
+        to_ring(0, way, 1, me, 0, first)
+    to_side(1, me, 0, first)
+    place = o_ref.at[side, part[1]]
+    move(place, place, side_send.at[0], side_recv.at[0], side).wait_recv()
+    for way in range(2):
+        to_ring(2, way, 1, side, 1)
+    for hop in range(1, 5):
+        for unit in (1, 0, 2):
+            for way in range(2):
+                if hop > hops[unit][way]:
+                    continue
+                source = lax.rem(row + (RING - hop if way == 0 else hop), RING)
+                origin = columns[unit] * RING + source
+                place = o_ref.at[origin, part[halves[unit]]]
+                at = (unit * 2 + way) * 4 + hop - 1
+                move(place, place, ring_send.at[at], ring_recv.at[at], ring[way]).wait_recv()
+                if hop < hops[unit][way]:
+                    to_ring(unit, way, hop + 1, origin, halves[unit])
+                if unit == 0:
+                    to_side(2 + way * 4 + hop - 1, origin, 0)
+    place = o_ref.at[side, part[0]]
+    move(place, place, side_send.at[1], side_recv.at[1], side).wait_recv()
+    for way in range(2):
+        for hop in range(1, hops[0][way] + 1):
+            source = lax.rem(row + (RING - hop if way == 0 else hop), RING)
+            place = o_ref.at[other * RING + source, part[0]]
+            slot = 2 + way * 4 + hop - 1
+            move(place, place, side_send.at[slot], side_recv.at[slot], side).wait_recv()
+    for copy in started:
+        copy.wait_send()
+    own.wait()
+
+
+def gather_rows(block, call):
+    total, width = block.shape
+    n_shard = lax.axis_size("fsdp")
+    whole = pl.pallas_call(
+        functools.partial(gather_kernel, total // 32 * 16),
+        out_shape=jax.ShapeDtypeStruct((n_shard, total, width), block.dtype),
+        in_specs=[pl.BlockSpec(memory_space=pltpu.VMEM)],
+        out_specs=pl.BlockSpec(memory_space=pltpu.VMEM),
+        scratch_shapes=[
+            pltpu.SemaphoreType.DMA((10,)),
+            pltpu.SemaphoreType.DMA((10,)),
+            pltpu.SemaphoreType.DMA((24,)),
+            pltpu.SemaphoreType.DMA((24,)),
+            pltpu.SemaphoreType.DMA,
+        ],
+        compiler_params=pltpu.CompilerParams(collective_id=call, has_side_effects=True),
+        cost_estimate=pl.CostEstimate(
+            flops=0, bytes_accessed=30 * n_shard * total * width, transcendentals=0
+        ),
+    )(block)
+    return whole.reshape(n_shard * total, width)
+
+
+def share_kernel(axis, count, x_ref, o_ref, slots, send, recv):
+    me = lax.axis_index(axis)
+    peers = [lax.rem(me + step, count) for step in range(1, count)]
+    barrier = pltpu.get_barrier_semaphore()
+    for peer in peers:
+        pl.semaphore_signal(barrier, inc=1, device_id={axis: peer}, device_id_type=MESH)
+    pl.semaphore_wait(barrier, count - 1)
+    copies = []
+    for at, peer in enumerate(peers):
+        copy = pltpu.make_async_remote_copy(
+            src_ref=x_ref,
+            dst_ref=slots.at[at],
+            send_sem=send.at[at],
+            recv_sem=recv.at[at],
+            device_id={axis: peer},
+            device_id_type=MESH,
+        )
+        copy.start()
+        copies.append(copy)
+    for copy in copies:
+        copy.wait()
+    o_ref[...] = x_ref[...] + jnp.sum(slots[...], axis=0)
+
+
+def summed_over(axis, tile, call):
+    count = lax.axis_size(axis)
+    return pl.pallas_call(
+        functools.partial(share_kernel, axis, count),
+        out_shape=jax.ShapeDtypeStruct(tile.shape, tile.dtype),
+        in_specs=[pl.BlockSpec(memory_space=pltpu.VMEM)],
+        out_specs=pl.BlockSpec(memory_space=pltpu.VMEM),
+        scratch_shapes=[
+            pltpu.VMEM((count - 1,) + tile.shape, tile.dtype),
+            pltpu.SemaphoreType.DMA((count - 1,)),
+            pltpu.SemaphoreType.DMA((count - 1,)),
+        ],
+        compiler_params=pltpu.CompilerParams(collective_id=call, has_side_effects=True),
+    )(tile)
 
 
 def local(tokens, cotangent, gain, master, momentum):
@@ -34,29 +196,34 @@
     cot = cotangent.astype(jnp.float32)
 
     normed = norm_rows(tokens, gain)
-    weights = lax.all_gather(master.astype(jnp.bfloat16), "fsdp", axis=0, tiled=True)
     mine = lax.dynamic_slice_in_dim(normed, lax.axis_index("dp") * share, share, 0)
-    some = lax.all_gather(mine, "fsdp", axis=0, tiled=True)
+    some = gather_rows(mine.reshape(-1, 128), 0).reshape(-1, normed.shape[1])
     gram = lax.dot_general(
         some, normed, along_features, preferred_element_type=jnp.float32
     ).astype(jnp.bfloat16)
     columns = lax.dynamic_slice_in_dim(some, lax.axis_index("fsdp") * own_rows, own_rows, 1)
-    both = lax.all_gather(jnp.concatenate([gram, columns], axis=1), "dp", axis=0, tiled=True)
+    piece, rounded = lax.optimization_barrier(
+        (jnp.concatenate([gram, columns], axis=1), master.astype(jnp.bfloat16))
+    )
+    both = lax.all_gather(piece, "dp", axis=0, tiled=True)
+    weights = gather_rows(rounded, 1)
     both = both.reshape(n_copy, n_shard, share, own_tokens + own_rows)
     both = both.transpose(1, 0, 2, 3).reshape(n_shard * own_tokens, own_tokens + own_rows)
     gram_all = both[:, :own_tokens]
     columns_all = both[:, own_tokens:]
 
-    def gathered(pre):
+    def gathered(pre, call):
         dpre = (cot * slope_of(pre)).astype(jnp.bfloat16)
-        return dpre, lax.all_gather(dpre, "fsdp", axis=0, tiled=True)
+        return dpre, gather_rows(dpre, call)
 
     pre = jnp.dot(normed, weights, preferred_element_type=jnp.float32)
-    dpre, dpre_all = gathered(pre)
+    dpre, dpre_all = gathered(pre, 2)
     shift = lax.dot_general(gram_all, dpre_all, along_rows, preferred_element_type=jnp.float32)
-    squares = lax.psum(jnp.sum(dpre.astype(jnp.float32) * shift), ("dp", "fsdp"))
+    products = (dpre.astype(jnp.float32) * shift).reshape(-1, 8, 128)
+    partial = summed_over("fsdp", jnp.sum(products, axis=0), 4)
+    squares = jnp.sum(summed_over("dp", partial, 5))
     scale = math.sqrt(FF) / 4.0 / (jnp.sqrt(jnp.maximum(squares, 0.0)) + 1e-12)
-    unused, dpre_two = gathered(pre + scale * shift)
+    unused, dpre_two = gathered(pre + scale * shift, 3)
     second = lax.dot_general(columns_all, dpre_two, along_rows, preferred_element_type=jnp.float32)
     new_momentum = 0.9 * momentum + second
     new_master = master - 0.002 * new_momentum

time: 541 us -> 289 us (0.53); the launches traced: 531 us -> 287 us
  waiting for transfers between devices: 341 us -> 45.6 us
  Pallas kernels: 0 us -> 155 us
  blocking collectives: 107 us -> 0 us
    all_gather x5 -> x1, waiting for transfers between devices: 341 us -> 45.6 us  [local(): both = lax.all_gather(piece, 'dp', axis=0, tiled=True)]
    pallas_call x0 -> x6, Pallas kernels: none -> 155 us  [the longest x4 130 us: gather_rows(): pl.pallas_call(functools.partial(gather_kernel, total // 32 * 16), out_sh...]
    psum x1 -> x0, blocking collectives: 107 us -> none  [local(): lax.psum(jnp.sum(dpre.astype(jnp.float32) * shift), ('dp', 'fsdp'))]
  transfers between devices with their start and end apart: 5 -> 1, of which waited for: 5 -> 1; matrix products, arithmetic and copies ran while one was open for 9% -> 2% of each run, Pallas kernels for 0% -> 24%
where the time goes in v1:
time: 289 us; the launch traced here: 287 us
  Pallas kernels  155 us (54%)
  waiting for transfers between devices  45.6 us (16%)
  local copies, waits for them, and re-layouts  41.4 us (14%)
  matrix products  19.4 us (7%)
  between operations  14.9 us (5%)
  other arithmetic  10.7 us (4%)
    pallas_call x4, Pallas kernels, gather_rows(): pl.pallas_call(functools.partial(gather_kernel, total // 32 * 16), out_sh...  130 us
    all_gather x1, waiting for transfers between devices, local(): both = lax.all_gather(piece, 'dp', axis=0, tiled=True)  45.6 us
    pallas_call x2, Pallas kernels, summed_over(): pl.pallas_call(functools.partial(share_kernel, axis, count), out_shape=ja...  24.9 us
    reshape x1, local copies, waits for them, and re-layouts, local(): both.transpose(1, 0, 2, 3)  13.6 us
    reshape x1, local copies, waits for them, and re-layouts, local(): both = both.reshape(n_copy, n_shard, share, own_tokens + own_rows)  12.8 us
    transpose x1, local copies, waits for them, and re-layouts, local(): both.transpose(1, 0, 2, 3)  9.21 us
    dot_general x1, matrix products, local(): lax.dot_general(columns_all, dpre_two, along_rows, preferred_element_type...  7.02 us
  transfers between devices with their start and end apart: 1, of which 1 were waited for; matrix products, arithmetic and copies ran while one was open for 2% of the time, Pallas kernels for 24%

profile of v1, /device:TPU:1, one launch (start us, length us, event | category | flops | bytes accessed | tf_op | source)
XLA Modules:
  0.0 286.5 jit_solution(18393123679900596950)
XLA Ops:
  7.2 2.5 fusion
  9.7 1.7 convert_element_type.27.x_ref
  11.5 2.7 fusion.2
  14.2 0.8 reshape.34.x_ref
  15.0 23.5 %shard_map.68 = bf16[16,360,128]{2,1,0:T(8,128)(2,1)} custom-call(bf16[360,128]{1,0:T(8,128)(2,1)} %reshape.34.x_ref), custom_call_target="tpu_custom_call" | custom-call | bytes 22118400 | tf_op jit(solution)/shard_map/pallas_call | solution.py:128
  38.5 4.0 %reshape_reshape.3 = bf16[160,4608]{1,0:T(8,128)(2,1)} reshape(bf16[16,360,128]{2,1,0:T(8,128)(2,1)} %shard_map.68) | data formatting | bytes 2949120 | tf_op jit(solution)/shard_map/reshape;reshape | solution.py:200
  42.5 2.6 convolution_convert_fusion
  45.1 1.0 constant_dynamic-slice_fusion
  46.1 0.8 pad_maximum_fusion
  46.9 30.9 %shard_map.69 = bf16[16,288,384]{2,1,0:T(8,128)(2,1)} custom-call(bf16[288,384]{1,0:T(8,128)(2,1)} %convert_element_type.27.x_ref), custom_call_target="tpu_custom_call" | custom-call | bytes 53084160 | tf_op jit(solution)/shard_map/pallas_call | solution.py:128
  77.8 4.5 %fusion.10 = (bf16[320,384]{1,0:T(8,128)(2,1)}, f32[320,384]{1,0:T(8,128)S(1)}) fusion(bf16[320,384]{1,0:T(8,128)(2,1)} %param.6, bf16[320,4608]{1,0:T(8,128)(2,1)S(1)} %fusion.2, bf16[4608,384]{1,0:T(8,128)(2,1)} %bitcast.13), kind=kOutput, calls=%fused_computation.15 | convolution fusion | flops 1133813760 | bytes 7471104 | tf_op jit(solution)/shard_map/dot_general | solution.py:219
  82.4 38.4 %shard_map.70 = bf16[16,320,384]{2,1,0:T(8,128)(2,1)} custom-call(bf16[320,384]{1,0:T(8,128)(2,1)} %get-tuple-element.6.x_ref), custom_call_target="tpu_custom_call" | custom-call | bytes 58982400 | tf_op jit(solution)/shard_map/pallas_call | solution.py:128
  120.7 45.6 %all-gather.2.cloned.1.call-done = bf16[5120,608]{1,0:T(8,128)(2,1)} async-done(((bf16[160,608]{1,0:T(8,128)(2,1)}), bf16[5120,608]{1,0:T(8,128)(2,1)}) %all-gather.2.cloned.1.call-update) | async-done | bytes 6225936 | tf_op jit(solution)/shard_map/all_gather | solution.py:208
  166.3 12.8 %reshape.35 = bf16[32,16,10,608]{3,2,1,0:T(8,128)(2,1)} reshape(bf16[5120,608]{1,0:T(8,128)(2,1)} %all-gather.2.cloned.1.call-done) | data formatting | bytes 12451840 | tf_op jit(solution)/shard_map/reshape | solution.py:210
  179.1 9.2 %copy.7 = bf16[16,32,10,608]{3,2,1,0:T(8,128)(2,1)} copy(bf16[16,32,10,608]{3,2,0,1:T(8,128)(2,1)} %bitcast.10) | data formatting | bytes 12451840 | tf_op jit(solution)/shard_map/transpose | solution.py:211
  188.3 13.6 %reshape.36 = bf16[5120,608]{1,0:T(8,128)(2,1)} reshape(bf16[16,32,10,608]{3,2,1,0:T(8,128)(2,1)} %copy.7) | data formatting | bytes 12451840 | tf_op jit(solution)/shard_map/reshape | solution.py:211
  201.9 5.2 %convert_multiply_fusion.4 = (f32[320,384]{1,0:T(8,128)S(1)}, f32[320,384]{1,0:T(8,128)S(1)}) fusion(bf16[320,384]{1,0:T(8,128)(2,1)S(1)} %copy-done.2, bf16[5120,384]{1,0:T(8,128)(2,1)} %bitcast.11, bf16[5120,608]{1,0:T(8,128)(2,1)} %reshape.36), kind=kOutput, calls=%fused_computation.25 | convolution fusion | flops 1258536960 | bytes 9093120 | tf_op jit(solution)/shard_map/dot_general | solution.py:221
  207.2 0.7 reduce_sum.28.x_ref
  207.9 9.9 %shard_map.71.x_ref = f32[8,128]{1,0:T(8,128)} custom-call(f32[8,128]{1,0:T(8,128)} %reduce_sum.28.x_ref), custom_call_target="tpu_custom_call" | custom-call | tf_op jit(solution)/shard_map/pallas_call | solution.py:174
  217.7 15.0 %shard_map.72 = f32[8,128]{1,0:T(8,128)} custom-call(f32[8,128]{1,0:T(8,128)} %shard_map.71.x_ref), custom_call_target="tpu_custom_call" | custom-call | tf_op jit(solution)/shard_map/pallas_call | solution.py:174
  232.7 1.3 reduce_sum.29
  234.8 1.0 fusion.11.x_ref
  235.7 36.9 %shard_map.73 = bf16[16,320,384]{2,1,0:T(8,128)(2,1)} custom-call(bf16[320,384]{1,0:T(8,128)(2,1)} %fusion.11.x_ref), custom_call_target="tpu_custom_call" | custom-call | bytes 58982400 | tf_op jit(solution)/shard_map/pallas_call | solution.py:128
  272.7 7.0 %multiply_subtract_fusion = (f32[288,384]{1,0:T(8,128)}, f32[288,384]{1,0:T(8,128)}) fusion(f32[288,384]{1,0:T(8,128)S(1)} %copy-done, bf16[5120,384]{1,0:T(8,128)(2,1)} %bitcast.12, bf16[5120,608]{1,0:T(8,128)(2,1)} %reshape.36, f32[288,384]{1,0:T(8,128)S(1)} %copy-done.3), kind=kOutput, calls=%fused_computation.26 | convolution fusion | flops 1132904448 | bytes 9633792 | tf_op jit(solution)/shard_map/dot_general | solution.py:227
  (13 shorter events, 0.2 us)
Async XLA Ops:
  7.2 159.1 %all-gather.2.cloned.1.call-start = ((), (), s32[]{:S(2)}) async-start(), calls=%async_computation | async-start | bytes 6758400 | tf_op jit(solution)/shard_map/all_gather | solution.py:208
  188.3 13.6 %copy-start.2 = (bf16[320,384]{1,0:T(8,128)(2,1)S(1)}, bf16[320,384]{1,0:T(8,128)(2,1)}, u32[]{:S(2)}) copy-start(bf16[320,384]{1,0:T(8,128)(2,1)} %get-tuple-element.6.x_ref) | copy-start | bytes 737284
  201.9 32.9 %copy-start.1 = (bf16[320,384]{1,0:T(8,128)(2,1)S(1)}, bf16[320,384]{1,0:T(8,128)(2,1)}, u32[]{:S(2)}) copy-start(bf16[320,384]{1,0:T(8,128)(2,1)} %param.6) | copy-start | bytes 737284
  207.1 65.5 %copy-start = (f32[288,384]{1,0:T(8,128)S(1)}, f32[288,384]{1,0:T(8,128)}, u32[]{:S(2)}) copy-start(f32[288,384]{1,0:T(8,128)} %param.8) | copy-start | bytes 1327108
  207.1 65.5 %copy-start.3 = (f32[288,384]{1,0:T(8,128)S(1)}, f32[288,384]{1,0:T(8,128)}, u32[]{:S(2)}) copy-start(f32[288,384]{1,0:T(8,128)} %param.9) | copy-start | bytes 1327108
Sparse Core Ops, SparseCore 0:
  47.0 119.2 all-gather.1

commit v2 on v1

--- a/solution.py
+++ b/solution.py
@@ -196,21 +196,46 @@
     cot = cotangent.astype(jnp.float32)
 
     normed = norm_rows(tokens, gain)
-    mine = lax.dynamic_slice_in_dim(normed, lax.axis_index("dp") * share, share, 0)
-    some = gather_rows(mine.reshape(-1, 128), 0).reshape(-1, normed.shape[1])
+    tall = share // 8 * 8
+    short = share - tall
+    position = lax.axis_index("dp")
+    mine = jnp.concatenate(
+        [
+            lax.dynamic_slice_in_dim(normed, position * tall, tall, 0),
+            lax.dynamic_slice_in_dim(normed, n_copy * tall + position * short, short, 0),
+        ]
+    )
+    some = gather_rows(mine.reshape(-1, 128), 0).reshape(n_shard, share, -1)
+    some = jnp.concatenate(
+        [
+            some[:, :tall].reshape(n_shard * tall, -1),
+            some[:, tall:].reshape(n_shard * short, -1),
+        ]
+    )
     gram = lax.dot_general(
         some, normed, along_features, preferred_element_type=jnp.float32
     ).astype(jnp.bfloat16)
     columns = lax.dynamic_slice_in_dim(some, lax.axis_index("fsdp") * own_rows, own_rows, 1)
-    piece, rounded = lax.optimization_barrier(
-        (jnp.concatenate([gram, columns], axis=1), master.astype(jnp.bfloat16))
-    )
-    both = lax.all_gather(piece, "dp", axis=0, tiled=True)
+
+    def in_token_order(whole):
+        whole = whole.reshape(n_copy, n_shard * share, -1)
+        width = whole.shape[2]
+
+        def swapped(rows, count):
+            rows = rows.reshape(n_copy, n_shard, count, width).transpose(1, 0, 2, 3)
+            return rows.reshape(n_shard, n_copy * count, width)
+
+        pieces = [
+            swapped(whole[:, : n_shard * tall], tall),
+            swapped(whole[:, n_shard * tall :], short),
+        ]
+        return jnp.concatenate(pieces, axis=1).reshape(n_shard * own_tokens, width)
+
+    gram, columns, rounded = lax.optimization_barrier(
+        (gram, columns, master.astype(jnp.bfloat16))
+    )
+    gram_all = lax.all_gather(gram, "dp", axis=0, tiled=True)
     weights = gather_rows(rounded, 1)
-    both = both.reshape(n_copy, n_shard, share, own_tokens + own_rows)
-    both = both.transpose(1, 0, 2, 3).reshape(n_shard * own_tokens, own_tokens + own_rows)
-    gram_all = both[:, :own_tokens]
-    columns_all = both[:, own_tokens:]
 
     def gathered(pre, call):
         dpre = (cot * slope_of(pre)).astype(jnp.bfloat16)
@@ -218,12 +243,16 @@
 
     pre = jnp.dot(normed, weights, preferred_element_type=jnp.float32)
     dpre, dpre_all = gathered(pre, 2)
+    columns, gram_all, dpre_all = lax.optimization_barrier((columns, gram_all, dpre_all))
+    columns_all = lax.all_gather(columns, "dp", axis=0, tiled=True)
+    gram_all = lax.optimization_barrier(in_token_order(gram_all))
     shift = lax.dot_general(gram_all, dpre_all, along_rows, preferred_element_type=jnp.float32)
     products = (dpre.astype(jnp.float32) * shift).reshape(-1, 8, 128)
-    partial = summed_over("fsdp", jnp.sum(products, axis=0), 4)
+    partial = summed_over("fsdp", jnp.sum(products, axis=(0, 1)).reshape(1, 128), 4)
     squares = jnp.sum(summed_over("dp", partial, 5))
     scale = math.sqrt(FF) / 4.0 / (jnp.sqrt(jnp.maximum(squares, 0.0)) + 1e-12)
     unused, dpre_two = gathered(pre + scale * shift, 3)
+    columns_all = lax.optimization_barrier(in_token_order(columns_all))
     second = lax.dot_general(columns_all, dpre_two, along_rows, preferred_element_type=jnp.float32)
     new_momentum = 0.9 * momentum + second
     new_master = master - 0.002 * new_momentum

time: 289 us -> 271 us (0.938)
  local copies, waits for them, and re-layouts: 41.4 us -> 19.3 us
  waiting for transfers between devices: 45.6 us -> 56.2 us
  matrix products: 19.4 us -> 12.9 us
    reshape x3 -> x7, local copies, waits for them, and re-layouts: 27.1 us -> 5.14 us  [the longest x4 3.21 us: swapped(): return rows.reshape(n_shard, n_copy * count, width)]
    all_gather x1 -> x2, waiting for transfers between devices: 45.6 us -> 56.2 us  [the longest x1 36.1 us: local(): gram_all = lax.all_gather(gram, 'dp', axis=0, tiled=True)]
    transpose x1 -> x2, local copies, waits for them, and re-layouts: 9.21 us -> 0.92 us  [swapped(): rows = rows.reshape(n_copy, n_shard, count, width).transpose(1, 0, 2, 3)]
    unnamed x8 -> x22, local copies, waits for them, and re-layouts: 0.02 us -> 5.08 us
    pallas_call x4, Pallas kernels: 130 us -> 135 us  [gather_rows(): pl.pallas_call(functools.partial(gather_kernel, total // 32 * 16), out_sh...]
    dot_general x1, matrix products: 7.02 us -> 2.65 us  [local(): lax.dot_general(columns_all, dpre_two, along_rows, preferred_element_type...]
    slice x0 -> x5, local copies, waits for them, and re-layouts: none -> 3.98 us  [the longest x4 3.11 us: in_token_order(): whole[:, n_shard * tall:]]
    dot_general x1, matrix products: 5.22 us -> 1.88 us  [local(): lax.dot_general(gram_all, dpre_all, along_rows, preferred_element_type=jn...]
  transfers between devices with their start and end apart: 1 -> 2, of which waited for: 1 -> 2; matrix products, arithmetic and copies ran while one was open for 2% -> 5% of each run, Pallas kernels for 24% -> 49%
where the time goes in v2:
time: 271 us
  Pallas kernels  157 us (58%)
  waiting for transfers between devices  56.2 us (21%)
  local copies, waits for them, and re-layouts  19.3 us (7%)
  between operations  15.1 us (6%)
  matrix products  12.9 us (5%)
  other arithmetic  9.69 us (4%)
    pallas_call x4, Pallas kernels, gather_rows(): pl.pallas_call(functools.partial(gather_kernel, total // 32 * 16), out_sh...  135 us
    all_gather x1, waiting for transfers between devices, local(): gram_all = lax.all_gather(gram, 'dp', axis=0, tiled=True)  36.1 us
    pallas_call x2, Pallas kernels, summed_over(): pl.pallas_call(functools.partial(share_kernel, axis, count), out_shape=ja...  22.7 us
    all_gather x1, waiting for transfers between devices, local(): columns_all = lax.all_gather(columns, 'dp', axis=0, tiled=True)  20.1 us
  transfers between devices with their start and end apart: 2, of which 2 were waited for; matrix products, arithmetic and copies ran while one was open for 5% of the time, Pallas kernels for 49%

profile of v2, /device:TPU:1, one launch (start us, length us, event | category | flops | bytes accessed | tf_op | source)
XLA Modules:
  0.0 270.7 jit_solution(9287730609785307653)
XLA Ops:
  7.2 2.7 fusion
  9.9 1.6 fusion.2
  11.5 1.7 copy-done.4
  14.9 23.5 %shard_map.68 = bf16[16,360,128]{2,1,0:T(8,128)(2,1)} custom-call(bf16[360,128]{1,0:T(8,128)(2,1)} %reshape.73.x_ref), custom_call_target="tpu_custom_call" | custom-call | bytes 22118400 | tf_op jit(solution)/shard_map/pallas_call | solution.py:128
  38.4 3.3 %reshape_reshape.3 = bf16[16,10,4608]{2,1,0:T(8,128)(2,1)S(1)} reshape(bf16[16,360,128]{2,1,0:T(8,128)(2,1)} %shard_map.68) | data formatting | bytes 2949120 | tf_op jit(solution)/shard_map/reshape;reshape | solution.py:208
  42.6 1.1 reshape.75
  43.7 3.8 %fusion.5 = bf16[160,320]{1,0:T(8,128)(2,1)} fusion(bf16[320,4608]{1,0:T(8,128)(2,1)} %copy-done.4, bf16[32,4608]{1,0:T(8,128)(2,1)S(1)} %reshape.75, bf16[128,4608]{1,0:T(8,128)(2,1)S(1)} %slice_bitcast_fusion.2), kind=kOutput, calls=%fused_computation.18 | convolution fusion | flops 474859520 | bytes 4526080 | tf_op jit(solution)/shard_map/dot_general | solution.py:215
  49.2 30.8 %shard_map.69 = bf16[16,288,384]{2,1,0:T(8,128)(2,1)} custom-call(bf16[288,384]{1,0:T(8,128)(2,1)} %convert_element_type.27.x_ref), custom_call_target="tpu_custom_call" | custom-call | bytes 53084160 | tf_op jit(solution)/shard_map/pallas_call | solution.py:128
  80.0 4.5 %fusion.6 = (bf16[320,384]{1,0:T(8,128)(2,1)}, f32[320,384]{1,0:T(8,128)S(1)}) fusion(bf16[320,384]{1,0:T(8,128)(2,1)} %param.6, bf16[320,4608]{1,0:T(8,128)(2,1)S(1)} %copy-done.5, bf16[4608,384]{1,0:T(8,128)(2,1)} %bitcast.47), kind=kOutput, calls=%fused_computation.23 | convolution fusion | flops 1133813760 | bytes 7471104 | tf_op jit(solution)/shard_map/dot_general | solution.py:244
  84.6 35.9 %shard_map.70 = bf16[16,320,384]{2,1,0:T(8,128)(2,1)} custom-call(bf16[320,384]{1,0:T(8,128)(2,1)} %get-tuple-element.14.x_ref), custom_call_target="tpu_custom_call" | custom-call | bytes 58982400 | tf_op jit(solution)/shard_map/pallas_call | solution.py:128
  120.5 36.1 %all-gather.3.cloned.1.call-done = bf16[5120,320]{1,0:T(8,128)(2,1)} async-done(((bf16[160,320]{1,0:T(8,128)(2,1)}), bf16[5120,320]{1,0:T(8,128)(2,1)}) %all-gather.3.cloned.1.call-update) | async-done | bytes 3276816 | tf_op jit(solution)/shard_map/all_gather | solution.py:237
  156.7 1.4 slice.29
  160.0 1.5 copy-done
  161.6 1.9 convert_multiply_fusion.4
  164.2 9.5 %shard_map.71.x_ref = f32[1,128]{1,0:T(1,128)} custom-call(f32[1,128]{1,0:T(1,128)} %bitcast.52), custom_call_target="tpu_custom_call" | custom-call | tf_op jit(solution)/shard_map/pallas_call | solution.py:174
  173.7 13.3 %shard_map.72 = f32[1,128]{1,0:T(1,128)} custom-call(f32[1,128]{1,0:T(1,128)} %shard_map.71.x_ref), custom_call_target="tpu_custom_call" | custom-call | tf_op jit(solution)/shard_map/pallas_call | solution.py:174
  186.9 1.3 reduce_sum.29
  188.9 1.0 fusion.7.x_ref
  189.9 44.4 %shard_map.73 = bf16[16,320,384]{2,1,0:T(8,128)(2,1)} custom-call(bf16[320,384]{1,0:T(8,128)(2,1)} %fusion.7.x_ref), custom_call_target="tpu_custom_call" | custom-call | bytes 58982400 | tf_op jit(solution)/shard_map/pallas_call | solution.py:128
  234.3 20.1 %all-gather.5.cloned.1.call-done = bf16[5120,288]{1,0:T(8,128)(2,1)} async-done(((bf16[160,288]{1,0:T(8,128)(2,1)}), bf16[5120,288]{1,0:T(8,128)(2,1)}) %all-gather.5.cloned.1.call-update) | async-done | bytes 2949136 | tf_op jit(solution)/shard_map/all_gather | solution.py:247
  254.3 1.2 slice.27
  255.6 2.4 copy_bitcast_fusion.1
  259.4 1.5 copy-done.3
  261.2 2.7 multiply_subtract_fusion
  (43 shorter events, 8.8 us)
Async XLA Ops:
  7.2 2.7 %copy-start.1 = (bf16[320,4608]{1,0:T(8,128)(2,1)S(1)}, bf16[320,4608]{1,0:T(8,128)(2,1)}, u32[]{:S(2)}) copy-start(bf16[320,4608]{1,0:T(8,128)(2,1)} %param.5) | copy-start | bytes 8847364
  7.2 149.4 %all-gather.3.cloned.1.call-start = ((), (), s32[]{:S(2)}) async-start(), calls=%async_computation | async-start | bytes 4055040 | tf_op jit(solution)/shard_map/all_gather | solution.py:237
  11.5 1.7 copy-start.4
  43.7 4.6 %copy-start.7 = (f32[288,384]{1,0:T(8,128)S(1)}, f32[288,384]{1,0:T(8,128)}, u32[]{:S(2)}) copy-start(f32[288,384]{1,0:T(8,128)} %param.8) | copy-start | bytes 1327108
  48.3 31.7 %copy-start.5 = (bf16[320,4608]{1,0:T(8,128)(2,1)S(1)}, bf16[320,4608]{1,0:T(8,128)(2,1)}, u32[]{:S(2)}) copy-start(bf16[320,4608]{1,0:T(8,128)(2,1)} %copy-done.4) | copy-start | bytes 8847364
  49.0 205.3 %all-gather.5.cloned.1.call-start = ((), (), s32[]{:S(2)}) async-start(), calls=%async_computation.1 | async-start | bytes 4055040 | tf_op jit(solution)/shard_map/all_gather | solution.py:247
  156.6 2.4 copy-start.2
  159.5 2.1 copy-start
  159.5 2.1 copy-start.6
  161.6 27.3 %copy-start.9 = (bf16[320,384]{1,0:T(8,128)(2,1)S(1)}, bf16[320,384]{1,0:T(8,128)(2,1)}, u32[]{:S(2)}) copy-start(bf16[320,384]{1,0:T(8,128)(2,1)} %param.6) | copy-start | bytes 737284
  258.9 2.1 copy-start.3
  258.9 2.2 copy-start.8
  258.9 2.3 copy-start.10
Sparse Core Ops, SparseCore 0:
  49.1 107.4 all-gather.2
  160.5 93.7 all-gather.4

commit v3 on v2

--- a/solution.py
+++ b/solution.py
@@ -231,10 +231,10 @@
         ]
         return jnp.concatenate(pieces, axis=1).reshape(n_shard * own_tokens, width)
 
-    gram, columns, rounded = lax.optimization_barrier(
-        (gram, columns, master.astype(jnp.bfloat16))
-    )
-    gram_all = lax.all_gather(gram, "dp", axis=0, tiled=True)
+    piece, rounded = lax.optimization_barrier(
+        (jnp.concatenate([gram, columns], axis=1), master.astype(jnp.bfloat16))
+    )
+    both = lax.all_gather(piece, "dp", axis=0, tiled=True)
     weights = gather_rows(rounded, 1)
 
     def gathered(pre, call):
@@ -243,16 +243,14 @@
 
     pre = jnp.dot(normed, weights, preferred_element_type=jnp.float32)
     dpre, dpre_all = gathered(pre, 2)
-    columns, gram_all, dpre_all = lax.optimization_barrier((columns, gram_all, dpre_all))
-    columns_all = lax.all_gather(columns, "dp", axis=0, tiled=True)
-    gram_all = lax.optimization_barrier(in_token_order(gram_all))
+    gram_all = lax.optimization_barrier(in_token_order(both[:, :own_tokens]))
     shift = lax.dot_general(gram_all, dpre_all, along_rows, preferred_element_type=jnp.float32)
     products = (dpre.astype(jnp.float32) * shift).reshape(-1, 8, 128)
     partial = summed_over("fsdp", jnp.sum(products, axis=(0, 1)).reshape(1, 128), 4)
     squares = jnp.sum(summed_over("dp", partial, 5))
     scale = math.sqrt(FF) / 4.0 / (jnp.sqrt(jnp.maximum(squares, 0.0)) + 1e-12)
     unused, dpre_two = gathered(pre + scale * shift, 3)
-    columns_all = lax.optimization_barrier(in_token_order(columns_all))
+    columns_all = lax.optimization_barrier(in_token_order(both[:, own_tokens:]))
     second = lax.dot_general(columns_all, dpre_two, along_rows, preferred_element_type=jnp.float32)
     new_momentum = 0.9 * momentum + second
     new_master = master - 0.002 * new_momentum

time: 271 us -> 265 us (0.978)
  waiting for transfers between devices: 56.2 us -> 45.5 us
  local copies, waits for them, and re-layouts: 19.3 us -> 24.8 us
  Pallas kernels: 157 us -> 153 us
    all_gather x2 -> x1, waiting for transfers between devices: 56.2 us -> 45.5 us  [local(): both = lax.all_gather(piece, 'dp', axis=0, tiled=True)]
    slice x0 -> x2, local copies, waits for them, and re-layouts: none -> 4.86 us  [the longest x1 2.66 us: local(): gram_all = lax.optimization_barrier(in_token_order(both[:, :own_tokens]))]
    pallas_call x4, Pallas kernels: 135 us -> 130 us  [gather_rows(): pl.pallas_call(functools.partial(gather_kernel, total // 32 * 16), out_sh...]
    unnamed x22 -> x24, local copies, waits for them, and re-layouts: 5.08 us -> 6.22 us
  transfers between devices with their start and end apart: 2 -> 1, of which waited for: 2 -> 1; matrix products, arithmetic and copies ran while one was open for 5% -> 2% of each run, Pallas kernels for 49% -> 26%
where the time goes in v3:
time: 265 us; the launch traced here: 263 us
  Pallas kernels  153 us (58%)
  waiting for transfers between devices  45.5 us (17%)
  local copies, waits for them, and re-layouts  24.8 us (9%)
  between operations  15.1 us (6%)
  matrix products  13.2 us (5%)
  other arithmetic  12 us (5%)
    pallas_call x4, Pallas kernels, gather_rows(): pl.pallas_call(functools.partial(gather_kernel, total // 32 * 16), out_sh...  130 us
    all_gather x1, waiting for transfers between devices, local(): both = lax.all_gather(piece, 'dp', axis=0, tiled=True)  45.5 us
    pallas_call x2, Pallas kernels, summed_over(): pl.pallas_call(functools.partial(share_kernel, axis, count), out_shape=ja...  22.7 us
    unnamed x24, local copies, waits for them, and re-layouts  6.22 us
  transfers between devices with their start and end apart: 1, of which 1 were waited for; matrix products, arithmetic and copies ran while one was open for 2% of the time, Pallas kernels for 26%

profile of v3, /device:TPU:1, one launch (start us, length us, event | category | flops | bytes accessed | tf_op | source)
XLA Modules:
  0.0 263.4 jit_solution(12145553624193539968)
XLA Ops:
  7.2 2.7 %fusion = f32[320]{0:T(512)S(1)} fusion(bf16[320,4608]{1,0:T(8,128)(2,1)} %param.5), kind=kLoop, calls=%fused_computation.2 | loop fusion | flops 4423360 | bytes 2950400 | tf_op jit(solution)/shard_map/reduce_sum | solution.py:20
  9.9 1.6 fusion.2
  11.5 1.6 copy-done.3
  14.8 23.5 %shard_map.68 = bf16[16,360,128]{2,1,0:T(8,128)(2,1)} custom-call(bf16[360,128]{1,0:T(8,128)(2,1)} %reshape.73.x_ref), custom_call_target="tpu_custom_call" | custom-call | bytes 22118400 | tf_op jit(solution)/shard_map/pallas_call | solution.py:128
  38.3 3.3 %reshape_reshape.3 = bf16[16,10,4608]{2,1,0:T(8,128)(2,1)S(1)} reshape(bf16[16,360,128]{2,1,0:T(8,128)(2,1)} %shard_map.68) | data formatting | bytes 2949120 | tf_op jit(solution)/shard_map/reshape;reshape | solution.py:208
  43.6 3.1 %fusion.5 = bf16[160,320]{1,0:T(8,128)(2,1)S(1)} fusion(bf16[320,4608]{1,0:T(8,128)(2,1)} %copy-done.3, bf16[32,4608]{1,0:T(8,128)(2,1)S(1)} %reshape.75, bf16[128,4608]{1,0:T(8,128)(2,1)S(1)} %slice_bitcast_fusion.2), kind=kOutput, calls=%fused_computation.18 | convolution fusion | flops 474859520 | bytes 4526080 | tf_op jit(solution)/shard_map/dot_general | solution.py:215
  48.4 31.1 %shard_map.69 = bf16[16,288,384]{2,1,0:T(8,128)(2,1)} custom-call(bf16[288,384]{1,0:T(8,128)(2,1)} %convert_element_type.27.x_ref), custom_call_target="tpu_custom_call" | custom-call | bytes 53084160 | tf_op jit(solution)/shard_map/pallas_call | solution.py:128
  79.5 4.6 %fusion.6 = (bf16[320,384]{1,0:T(8,128)(2,1)}, f32[320,384]{1,0:T(8,128)}) fusion(bf16[320,384]{1,0:T(8,128)(2,1)S(1)} %copy-done.8, bf16[320,4608]{1,0:T(8,128)(2,1)S(1)} %copy-done.4, bf16[4608,384]{1,0:T(8,128)(2,1)} %bitcast.49), kind=kOutput, calls=%fused_computation.23 | convolution fusion | flops 1133813760 | bytes 7471104 | tf_op jit(solution)/shard_map/dot_general | solution.py:244
  84.1 38.4 %shard_map.70 = bf16[16,320,384]{2,1,0:T(8,128)(2,1)} custom-call(bf16[320,384]{1,0:T(8,128)(2,1)} %get-tuple-element.6.x_ref), custom_call_target="tpu_custom_call" | custom-call | bytes 58982400 | tf_op jit(solution)/shard_map/pallas_call | solution.py:128
  122.5 45.5 %all-gather.2.cloned.1.call-done = bf16[5120,608]{1,0:T(8,128)(2,1)} async-done(((bf16[160,608]{1,0:T(8,128)(2,1)}), bf16[5120,608]{1,0:T(8,128)(2,1)}) %all-gather.2.cloned.1.call-update) | async-done | bytes 6225936 | tf_op jit(solution)/shard_map/all_gather | solution.py:237
  168.0 2.7 %slice.37 = bf16[5120,320]{1,0:T(8,128)(2,1)S(1)} slice(bf16[5120,608]{1,0:T(8,128)(2,1)} %all-gather.2.cloned.1.call-done), slice={[0:5120], [0:320]} | slice | bytes 6553600 | tf_op jit(solution)/shard_map/slice | solution.py:246
  172.5 2.2 slice.34
  177.6 1.5 copy-done
  179.2 2.8 %convert_multiply_fusion.4 = (f32[320,384]{1,0:T(8,128)}, f32[320,384]{1,0:T(8,128)}) fusion(bf16[320,384]{1,0:T(8,128)(2,1)S(1)} %copy-done.5, bf16[5120,320]{1,0:T(8,128)(2,1)S(1)} %bitcast.40, bf16[5120,384]{1,0:T(8,128)(2,1)S(1)} %bitcast.39), kind=kOutput, calls=%fused_computation.33 | convolution fusion | flops 1258536960 | bytes 8437760 | tf_op jit(solution)/shard_map/dot_general | solution.py:247
  182.0 1.9 reshape.90
  183.9 1.7 reduce_sum.28
  185.6 9.5 %shard_map.71.x_ref = f32[1,128]{1,0:T(1,128)} custom-call(f32[1,128]{1,0:T(1,128)} %bitcast.54), custom_call_target="tpu_custom_call" | custom-call | tf_op jit(solution)/shard_map/pallas_call | solution.py:174
  195.1 13.2 %shard_map.72 = f32[1,128]{1,0:T(1,128)} custom-call(f32[1,128]{1,0:T(1,128)} %shard_map.71.x_ref), custom_call_target="tpu_custom_call" | custom-call | tf_op jit(solution)/shard_map/pallas_call | solution.py:174
  208.3 1.2 reduce_sum.29
  210.3 2.1 fusion.7.x_ref
  212.4 37.2 %shard_map.73 = bf16[16,320,384]{2,1,0:T(8,128)(2,1)} custom-call(bf16[320,384]{1,0:T(8,128)(2,1)} %fusion.7.x_ref), custom_call_target="tpu_custom_call" | custom-call | bytes 58982400 | tf_op jit(solution)/shard_map/pallas_call | solution.py:128
  249.6 1.4 copy.10
  252.2 1.5 copy-done.2
  254.0 2.6 %multiply_subtract_fusion = (f32[288,384]{1,0:T(8,128)}, f32[288,384]{1,0:T(8,128)}) fusion(f32[288,384]{1,0:T(8,128)S(1)} %copy-done.7, bf16[5120,288]{1,0:T(8,128)(2,1)S(1)} %bitcast.48, bf16[5120,384]{1,0:T(8,128)(2,1)S(1)} %bitcast.47, f32[288,384]{1,0:T(8,128)S(1)} %copy-done.9), kind=kOutput, calls=%fused_computation.34 | convolution fusion | flops 1132904448 | bytes 8650752 | tf_op jit(solution)/shard_map/dot_general | solution.py:254
  (46 shorter events, 11.6 us)
Async XLA Ops:
  7.2 2.7 %copy-start.1 = (bf16[320,4608]{1,0:T(8,128)(2,1)S(1)}, bf16[320,4608]{1,0:T(8,128)(2,1)}, u32[]{:S(2)}) copy-start(bf16[320,4608]{1,0:T(8,128)(2,1)} %param.5) | copy-start | bytes 8847364
  7.2 160.8 %all-gather.2.cloned.1.call-start = ((), (), s32[]{:S(2)}) async-start(), calls=%async_computation | async-start | bytes 6758400 | tf_op jit(solution)/shard_map/all_gather | solution.py:237
  11.5 1.6 copy-start.3
  43.6 3.3 %copy-start.6 = (f32[288,384]{1,0:T(8,128)S(1)}, f32[288,384]{1,0:T(8,128)}, u32[]{:S(2)}) copy-start(f32[288,384]{1,0:T(8,128)} %param.8) | copy-start | bytes 1327108
  46.7 32.8 %copy-start.8 = (bf16[320,384]{1,0:T(8,128)(2,1)S(1)}, bf16[320,384]{1,0:T(8,128)(2,1)}, u32[]{:S(2)}) copy-start(bf16[320,384]{1,0:T(8,128)(2,1)} %param.6) | copy-start | bytes 737284
  46.9 32.6 %copy-start.4 = (bf16[320,4608]{1,0:T(8,128)(2,1)S(1)}, bf16[320,4608]{1,0:T(8,128)(2,1)}, u32[]{:S(2)}) copy-start(bf16[320,4608]{1,0:T(8,128)(2,1)} %copy-done.3) | copy-start | bytes 8847364
  168.0 3.4 %slice-start = ((s8[6553600]{0:T(1024)(128)(4,1)}), s8[4194304]{0:T(1024)(128)(4,1)S(1)}, s32[]{:S(2)}) async-start(s8[6553600]{0:T(1024)(128)(4,1)} %bitcast.45), calls=%async_computation.1 | async-start | bytes 8388608
  170.7 1.8 slice-start.1
  177.1 2.1 copy-start
  177.1 2.1 copy-start.5
  251.6 2.1 copy-start.2
  251.6 2.2 copy-start.7
  251.6 2.3 copy-start.9
Sparse Core Ops, SparseCore 0:
  48.6 119.3 all-gather.1
